TPU v7x, 512 devices: a whole 4x4x16 slice. The times are simulated.
512 devices in a mesh: dp: 64 (over z, y), sub: 8 (over x, core).
Axes of the slice: x: 4, y: 4, z: 16, core: 2. Of those that a mesh axis runs over, the one named last changes fastest.
Arguments:
- embeddings: bfloat16 [524288, 1024], P(('dp', 'sub')), may hold values from -6 to 6
- cluster_of: int32 [524288], P(('dp', 'sub')), may hold values from 0 to 1087, as said below
Outputs:
- density: float32 [524288], P(('dp', 'sub'))
Inputs may be any that keep to these rules, and one draw needn't show every extreme that they name: `cluster_of`: A cluster c < 2 * 512 is held whole by the device of dp index (c // 2) // 8 and sub index (c // 2) % 8; a cluster c >= 2 * 512 is spread over the sub devices of dp index (c - 2 * 512). Of one device's rows exactly 896 lie in whole-held clusters and 128 in spread ones. At most 3 of one device's rows lie in the whole-held clusters of one device; one device gets exactly 3 such rows from every device. At most 4 of one device's rows lie in the spread clusters of one dp index; one dp index gets exactly 4 such rows from every device.
All inputs are finite; a program needn't handle non-finite values.
Results may differ from a plain program's by a relative error of at most 0.0005.
The roundings to bfloat16 on the way count: a program that leaves them out, or rounds other values in their place, can miss the bound.
Values may be sent and summed in bfloat16 or wider, within the bound.
A program may use at most 64 MiB of HBM per device.

v0:
```python
import jax
import jax.numpy as jnp
from jax import lax
from jax.sharding import PartitionSpec as P

SC = 2
LC = 1
kernel_scale = 32.0


def unit_norm(values):
    floats = values.astype(jnp.float32)
    scaled = floats * lax.rsqrt(jnp.sum(floats * floats, axis=1, keepdims=True) + 1e-06)
    return scaled.astype(jnp.bfloat16)


def pair_terms(left_rows, left_ids, left_place, right_rows, right_ids, right_place):
    similar = lax.dot_general(
        left_rows, right_rows, (((1,), (1,)), ((), ())), preferred_element_type=jnp.float32
    )
    same_cluster = (left_ids[:, None] == right_ids[None, :]) & (left_ids[:, None] >= 0)
    keep_pair = same_cluster & (left_place[:, None] != right_place[None, :])
    weights = jnp.where(keep_pair, jnp.exp(kernel_scale * similar), 0.0)
    return (weights, same_cluster.astype(jnp.float32))


def rank_within(labels):
    length = labels.shape[0]
    places = jnp.arange(length, dtype=jnp.int32)
    earlier = places[None, :] < places[:, None]
    matches = (labels[:, None] == labels[None, :]) & earlier
    return jnp.sum(matches.astype(jnp.int32), axis=1)


def finish(kernel_mass, members, labels):
    return jnp.where(labels >= 0, kernel_mass / jnp.maximum(members, 1.0), 0.0)


def local(embeddings, cluster_of):
    dp_count = lax.axis_size("dp")
    sub_count = lax.axis_size("sub")
    device_count = dp_count * sub_count
    local_rows = embeddings.shape[0]
    feature_width = embeddings.shape[1]
    spread_count = local_rows // 8
    planned_count = local_rows - spread_count
    small_cap = max(2, (3 * planned_count + 2 * device_count - 1) // (2 * device_count))
    large_cap = max(2, (2 * spread_count + dp_count - 1) // dp_count)
    unit_rows = unit_norm(embeddings)
    whole_count = SC * device_count
    planned = cluster_of < whole_count
    holder_of = cluster_of // SC
    owners = jnp.where(planned, holder_of // sub_count, (cluster_of - whole_count) // LC)
    tile_of = jnp.where(planned, holder_of % sub_count, -1)
    target = owners * sub_count + tile_of
    small_label = jnp.where(planned, target, -1)
    large_label = jnp.where(planned, -1, owners)
    small_slot = jnp.where(
        planned, target * small_cap + rank_within(small_label), device_count * small_cap
    )
    large_slot = jnp.where(
        planned, dp_count * large_cap, owners * large_cap + rank_within(large_label)
    )
    small_send = (
        jnp.zeros((device_count * small_cap, feature_width), jnp.bfloat16)
        .at[small_slot]
        .set(unit_rows, mode="drop")
    )
    small_send = small_send.reshape(dp_count, sub_count, small_cap, feature_width)
    small_tags = (
        jnp.full((device_count * small_cap,), -1, jnp.int32)
        .at[small_slot]
        .set(cluster_of, mode="drop")
    )
    small_tags = small_tags.reshape(dp_count, sub_count, small_cap)
    large_send = (
        jnp.zeros((dp_count * large_cap, feature_width), jnp.bfloat16)
        .at[large_slot]
        .set(unit_rows, mode="drop")
    )
    large_send = large_send.reshape(dp_count, large_cap, feature_width)
    large_tags = (
        jnp.full((dp_count * large_cap,), -1, jnp.int32).at[large_slot].set(cluster_of, mode="drop")
    )
    large_tags = large_tags.reshape(dp_count, large_cap)
    got_rows, got_tags = (
        lax.all_to_all(
            lax.all_to_all(small_send, "dp", split_axis=0, concat_axis=0, tiled=True),
            "sub",
            split_axis=1,
            concat_axis=1,
            tiled=True,
        ),
        lax.all_to_all(
            lax.all_to_all(small_tags, "dp", split_axis=0, concat_axis=0, tiled=True),
            "sub",
            split_axis=1,
            concat_axis=1,
            tiled=True,
        ),
    )
    got_large, got_large_tags = (
        lax.all_to_all(large_send, "dp", split_axis=0, concat_axis=0, tiled=True),
        lax.all_to_all(large_tags, "dp", split_axis=0, concat_axis=0, tiled=True),
    )
    planned_flat = got_rows.reshape(-1, feature_width)
    planned_ids = got_tags.reshape(-1)
    slot_total = planned_flat.shape[0]
    block_size = 512
    all_places = jnp.arange(slot_total, dtype=jnp.int32)

    def planned_block(block_index):
        block_start = block_index * block_size
        part_rows = lax.dynamic_slice_in_dim(planned_flat, block_start, block_size, 0)
        part_ids = lax.dynamic_slice_in_dim(planned_ids, block_start, block_size, 0)
        part_places = block_start + jnp.arange(block_size, dtype=jnp.int32)
        weights, same_cluster = pair_terms(
            part_rows, part_ids, part_places, planned_flat, planned_ids, all_places
        )
        return finish(jnp.sum(weights, axis=1), jnp.sum(same_cluster, axis=1), part_ids)

    planned_density = lax.map(planned_block, jnp.arange(slot_total // block_size, dtype=jnp.int32))
    planned_density = planned_density.reshape(dp_count, sub_count, small_cap)
    spread_flat = got_large.reshape(-1, feature_width)
    spread_ids = got_large_tags.reshape(-1)
    spread_total = spread_flat.shape[0]
    places = jnp.arange(spread_total, dtype=jnp.int32)
    my_places = lax.axis_index("sub") * spread_total + places
    piece_rows = lax.all_gather(spread_flat, "sub", axis=0, tiled=True)
    piece_ids = lax.all_gather(spread_ids, "sub", axis=0, tiled=True)
    piece_places = jnp.arange(piece_rows.shape[0], dtype=jnp.int32)
    weights, same_cluster = pair_terms(
        spread_flat, spread_ids, my_places, piece_rows, piece_ids, piece_places
    )
    kernel_mass = jnp.sum(weights, axis=1)
    members = jnp.sum(same_cluster, axis=1)
    spread_density = finish(kernel_mass, members, spread_ids).reshape(dp_count, large_cap)
    back_planned = lax.all_to_all(
        lax.all_to_all(planned_density, "dp", split_axis=0, concat_axis=0, tiled=True),
        "sub",
        split_axis=1,
        concat_axis=1,
        tiled=True,
    )
    back_spread = lax.all_to_all(spread_density, "dp", split_axis=0, concat_axis=0, tiled=True)
    from_planned = jnp.take(back_planned.reshape(-1), small_slot, mode="clip")
    from_spread = jnp.take(back_spread.reshape(-1), large_slot, mode="clip")
    return jnp.where(planned, from_planned, from_spread)


def solution(mesh):
    placed = (P(("dp", "sub"), None), P(("dp", "sub")))
    return jax.shard_map(
        local, mesh=mesh, in_specs=placed, out_specs=P(("dp", "sub")), check_vma=False
    )
```

profile of v0, /device:TPU:1, one launch (start us, length us, event | category | flops | bytes accessed | tf_op | source)
XLA Modules:
  0.0 422.4 jit_solution(3138771682105180316)
XLA Ops:
  13.8 19.3 %all-to-all-start.6 = ((s32[64,1,4]{2,1,0:T(1,128)}), s32[64,1,4]{2,1,0:T(1,128)S(1)}, u32[]{:S(2)}, u32[]{:S(2)}) async-start(s32[64,1,4]{2,1,0:T(1,128)} %bitcast), calls=%async_computation.6 | async-start | bytes 65536 | tf_op jit(solution)/shard_map/all_to_all | solution.py:104
  41.5 5.2 %all-to-all-done.6 = s32[64,1,4]{2,1,0:T(1,128)S(1)} async-done(((s32[64,1,4]{2,1,0:T(1,128)}), s32[64,1,4]{2,1,0:T(1,128)S(1)}, u32[]{:S(2)}, u32[]{:S(2)}) %all-to-all-start.6) | async-done | bytes 1056 | tf_op jit(solution)/shard_map/all_to_all | solution.py:104
  46.7 9.3 %all-to-all-start = ((s32[64,8,3]{1,2,0:T(4,128)}), s32[64,8,3]{1,2,0:T(4,128)S(1)}, u32[]{:S(2)}, u32[]{:S(2)}) async-start(s32[64,8,3]{1,2,0:T(4,128)} %copy.16), calls=%async_computation | async-start | bytes 262144 | tf_op jit(solution)/shard_map/all_to_all | solution.py:95
  56.0 5.7 %scatter_custom_fusion.3 = bf16[256,1024]{1,0:T(8,128)(2,1)S(1)} fusion(s32[1024]{0:T(1024)S(1)} %get-tuple-element.88, bf16[1024,1024]{1,0:T(8,128)(2,1)S(1)} %copy-done, f32[1024]{0:T(1024)S(1)} %add_rsqrt_fusion, bf16[]{:T(256)} %constant.90.clone.1), kind=kCustom, calls=%fused_computation.40 | custom fusion | flops 3145728 | bytes 2625538 | tf_op jit(solution)/shard_map/scatter | solution.py:79
  62.7 8.4 %all-to-all-done = s32[64,8,3]{1,2,0:T(4,128)S(1)} async-done(((s32[64,8,3]{1,2,0:T(4,128)}), s32[64,8,3]{1,2,0:T(4,128)S(1)}, u32[]{:S(2)}, u32[]{:S(2)}) %all-to-all-start) | async-done | bytes 6176 | tf_op jit(solution)/shard_map/all_to_all | solution.py:95
  71.1 6.4 %all-to-all-start.7 = ((bf16[64,4,1024]{2,1,0:T(4,128)(2,1)}), bf16[64,4,1024]{2,1,0:T(4,128)(2,1)S(1)}, u32[]{:S(2)}, u32[]{:S(2)}) async-start(bf16[64,4,1024]{2,1,0:T(4,128)(2,1)} %reshape.104), calls=%async_computation.7 | async-start | bytes 1048576 | tf_op jit(solution)/shard_map/all_to_all | solution.py:103
  77.5 7.8 %scatter_custom_fusion.1 = bf16[1536,1024]{1,0:T(8,128)(2,1)} fusion(s32[1024]{0:T(1024)S(1)} %get-tuple-element.90, bf16[]{:T(256)} %constant.90.clone.1, bf16[1024,1024]{1,0:T(8,128)(2,1)S(1)} %copy-done, f32[1024]{0:T(1024)S(1)} %add_rsqrt_fusion), kind=kCustom, calls=%fused_computation.37 | custom fusion | flops 3145728 | bytes 5246978 | tf_op jit(solution)/shard_map/scatter | solution.py:67
  85.3 9.1 %reshape.100 = bf16[64,8,3,1024]{3,2,1,0:T(4,128)(2,1)} reshape(bf16[1536,1024]{1,0:T(8,128)(2,1)} %scatter_custom_fusion.1) | data formatting | bytes 6291456 | tf_op jit(solution)/shard_map/reshape | solution.py:69
  94.4 5.6 %copy.19 = bf16[64,8,3,1024]{3,1,2,0:T(8,128)(2,1)} copy(bf16[64,8,3,1024]{3,2,1,0:T(4,128)(2,1)} %reshape.100) | data formatting | bytes 6291456 | tf_op jit(solution)/shard_map/reshape | solution.py:69
  100.0 6.3 %all-to-all-done.7 = bf16[64,4,1024]{2,1,0:T(4,128)(2,1)S(1)} async-done(((bf16[64,4,1024]{2,1,0:T(4,128)(2,1)}), bf16[64,4,1024]{2,1,0:T(4,128)(2,1)S(1)}, u32[]{:S(2)}, u32[]{:S(2)}) %all-to-all-start.7) | async-done | bytes 524320 | tf_op jit(solution)/shard_map/all_to_all | solution.py:103
  107.0 8.9 %all-to-all-start.2 = ((bf16[64,8,3,1024]{3,1,2,0:T(8,128)(2,1)}), bf16[64,8,3,1024]{3,1,2,0:T(8,128)(2,1)S(1)}, u32[]{:S(2)}, u32[]{:S(2)}) async-start(bf16[64,8,3,1024]{3,1,2,0:T(8,128)(2,1)} %copy.19), calls=%async_computation.2 | async-start | bytes 6291456 | tf_op jit(solution)/shard_map/all_to_all | solution.py:88
  118.8 135.5 %all-to-all-done.2 = bf16[64,8,3,1024]{3,1,2,0:T(8,128)(2,1)S(1)} async-done(((bf16[64,8,3,1024]{3,1,2,0:T(8,128)(2,1)}), bf16[64,8,3,1024]{3,1,2,0:T(8,128)(2,1)S(1)}, u32[]{:S(2)}, u32[]{:S(2)}) %all-to-all-start.2) | async-done | bytes 3145760 | tf_op jit(solution)/shard_map/all_to_all | solution.py:88
  254.3 12.1 %all-to-all-start.1 = ((s32[8,1,192]{2,1,0:T(1,128)}), s32[8,1,192]{2,1,0:T(1,128)S(1)}, u32[]{:S(2)}, u32[]{:S(2)}) async-start(s32[8,1,192]{2,1,0:T(1,128)} %reshape.193), calls=%async_computation.1 | async-start | bytes 16384 | tf_op jit(solution)/shard_map/all_to_all | solution.py:94
  276.7 39.7 %all-gather = s32[8,1,256]{2,1,0:T(1,128)S(1)} all-gather(s32[1,1,256]{2,1,0:T(1,128)S(1)} %reshape.161), channel_id=1, replica_groups=mesh['dp'=64,'sub'=8] {'sub'}, dimensions={0}, use_global_device_ids=true | all-gather | bytes 9216 | tf_op jit(solution)/shard_map/all_gather | solution.py:130
  323.3 4.6 %copy.21 = bf16[64,8,3,1024]{3,2,1,0:T(4,128)(2,1)} copy(bf16[64,8,3,1024]{3,0,2,1:T(8,128)(2,1)S(1)} %all-to-all-done.3) | data formatting | bytes 6291456 | tf_op jit(solution)/shard_map/all_to_all | solution.py:87
  327.9 7.5 %reshape.101 = bf16[1536,1024]{1,0:T(8,128)(2,1)S(1)} reshape(bf16[64,8,3,1024]{3,2,1,0:T(4,128)(2,1)} %copy.21) | data formatting | bytes 6291456 | tf_op jit(solution)/shard_map/reshape | solution.py:106
  335.4 15.6 %while.12 = (s32[]{:T(128)}, f32[3,512]{1,0:T(4,128)S(1)}, s32[3]{0:T(128)S(1)}, s32[1536]{0:T(1024)S(1)}, s32[64,8,3]{2,1,0:T(8,128)}, /*index=5*/bf16[1536,102...) while((s32[]{:T(128)}, f32[3,512]{1,0:T(4,128)S(1)}, ...), condition=%wide.wide.region_7.8_spmd.clone, body=%wide.wide.region_4.7_spmd.clone.sunk | while | flops 1619265024 | bytes 4237495 | solution.py:122
  352.3 5.6 %all-to-all-start.4 = ((f32[64,8,3]{1,2,0:T(4,128)}), f32[64,8,3]{1,2,0:T(4,128)S(1)}, u32[]{:S(2)}, u32[]{:S(2)}) async-start(f32[64,8,3]{1,2,0:T(4,128)} %copy.23), calls=%async_computation.4 | async-start | bytes 262144 | tf_op jit(solution)/shard_map/all_to_all | solution.py:139
  358.5 15.0 %all-to-all-done.4 = f32[64,8,3]{1,2,0:T(4,128)S(1)} async-done(((f32[64,8,3]{1,2,0:T(4,128)}), f32[64,8,3]{1,2,0:T(4,128)S(1)}, u32[]{:S(2)}, u32[]{:S(2)}) %all-to-all-start.4) | async-done | bytes 6176 | tf_op jit(solution)/shard_map/all_to_all | solution.py:139
  373.5 5.8 %all-to-all-start.8 = ((f32[64,1,4]{2,1,0:T(1,128)}), f32[64,1,4]{2,1,0:T(1,128)S(1)}, u32[]{:S(2)}, u32[]{:S(2)}) async-start(f32[64,1,4]{2,1,0:T(1,128)} %bitcast.3), calls=%async_computation.8 | async-start | bytes 65536 | tf_op jit(solution)/shard_map/all_to_all | solution.py:145
  380.1 12.8 %all-to-all-done.8 = f32[64,1,4]{2,1,0:T(1,128)S(1)} async-done(((f32[64,1,4]{2,1,0:T(1,128)}), f32[64,1,4]{2,1,0:T(1,128)S(1)}, u32[]{:S(2)}, u32[]{:S(2)}) %all-to-all-start.8) | async-done | bytes 1056 | tf_op jit(solution)/shard_map/all_to_all | solution.py:145
  392.9 6.0 %all-to-all-start.5 = ((f32[8,1,192]{2,1,0:T(1,128)}), f32[8,1,192]{2,1,0:T(1,128)S(1)}, u32[]{:S(2)}, u32[]{:S(2)}) async-start(f32[8,1,192]{2,1,0:T(1,128)} %reshape.195), calls=%async_computation.5 | async-start | bytes 16384 | tf_op jit(solution)/shard_map/all_to_all | solution.py:138
  400.3 6.8 %gather_fusion.1 = f32[1024]{0:T(1024)S(1)} fusion(f32[256]{0:T(256)S(1)} %reshape.106, s32[1024]{0:T(1024)S(1)} %get-tuple-element.87), kind=kCustom, calls=%fused_computation.1 | custom fusion | bytes 12288 | tf_op jit(solution)/shard_map/jit(_take)/gather | solution.py:147
  408.8 6.2 %gather_fusion = f32[1024]{0:T(1024)S(1)} fusion(f32[1536]{0:T(1024)S(1)} %reshape.103, s32[1024]{0:T(1024)S(1)} %get-tuple-element.89), kind=kCustom, calls=%fused_computation | custom fusion | bytes 12288 | tf_op jit(solution)/shard_map/jit(_take)/gather | solution.py:146
  (83 shorter events, 56.9 us)
Async XLA Ops:
  6.5 49.5 %copy-start = (bf16[1024,1024]{1,0:T(8,128)(2,1)S(1)}, bf16[1024,1024]{1,0:T(8,128)(2,1)}, u32[]{:S(2)}) copy-start(bf16[1024,1024]{1,0:T(8,128)(2,1)} %param.4) | copy-start | bytes 6291460
  13.8 32.9 %all-to-all-start.6 = ((s32[64,1,4]{2,1,0:T(1,128)}), s32[64,1,4]{2,1,0:T(1,128)S(1)}, u32[]{:S(2)}, u32[]{:S(2)}) async-start(s32[64,1,4]{2,1,0:T(1,128)} %bitcast), calls=%async_computation.6 | async-start | bytes 65536 | tf_op jit(solution)/shard_map/all_to_all | solution.py:104
  46.7 24.4 %all-to-all-start = ((s32[64,8,3]{1,2,0:T(4,128)}), s32[64,8,3]{1,2,0:T(4,128)S(1)}, u32[]{:S(2)}, u32[]{:S(2)}) async-start(s32[64,8,3]{1,2,0:T(4,128)} %copy.16), calls=%async_computation | async-start | bytes 262144 | tf_op jit(solution)/shard_map/all_to_all | solution.py:95
  71.1 35.1 %all-to-all-start.7 = ((bf16[64,4,1024]{2,1,0:T(4,128)(2,1)}), bf16[64,4,1024]{2,1,0:T(4,128)(2,1)S(1)}, u32[]{:S(2)}, u32[]{:S(2)}) async-start(bf16[64,4,1024]{2,1,0:T(4,128)(2,1)} %reshape.104), calls=%async_computation.7 | async-start | bytes 1048576 | tf_op jit(solution)/shard_map/all_to_all | solution.py:103
  106.2 0.8 copy-start.2
  107.0 147.2 %all-to-all-start.2 = ((bf16[64,8,3,1024]{3,1,2,0:T(8,128)(2,1)}), bf16[64,8,3,1024]{3,1,2,0:T(8,128)(2,1)S(1)}, u32[]{:S(2)}, u32[]{:S(2)}) async-start(bf16[64,8,3,1024]{3,1,2,0:T(8,128)(2,1)} %copy.19), calls=%async_computation.2 | async-start | bytes 6291456 | tf_op jit(solution)/shard_map/all_to_all | solution.py:88
  116.0 202.9 %all-gather.3.cloned.1.call-start = ((), (), s32[]{:S(2)}) async-start(), calls=%async_computation.9 | async-start | bytes 4718592 | tf_op jit(solution)/shard_map/all_gather | solution.py:129
  254.3 16.7 %all-to-all-start.1 = ((s32[8,1,192]{2,1,0:T(1,128)}), s32[8,1,192]{2,1,0:T(1,128)S(1)}, u32[]{:S(2)}, u32[]{:S(2)}) async-start(s32[8,1,192]{2,1,0:T(1,128)} %reshape.193), calls=%async_computation.1 | async-start | bytes 16384 | tf_op jit(solution)/shard_map/all_to_all | solution.py:94
  271.0 52.3 %all-to-all-start.3 = ((bf16[64,8,3,1024]{3,0,2,1:T(8,128)(2,1)}), bf16[64,8,3,1024]{3,0,2,1:T(8,128)(2,1)S(1)}, u32[]{:S(2)}, u32[]{:S(2)}) async-start(bf16[64,8,3,1024]{3,0,2,1:T(8,128)(2,1)} %copy.20), calls=%async_computation.3 | async-start | bytes 6291456 | tf_op jit(solution)/shard_map/all_to_all | solution.py:87
  318.5 4.7 %copy-start.1 = (s32[64,8,3]{2,1,0:T(8,128)}, s32[64,8,3]{2,1,0:T(8,128)S(1)}, u32[]{:S(2)}) copy-start(s32[64,8,3]{2,1,0:T(8,128)S(1)} %copy.18) | copy-start | bytes 18436
  352.3 21.2 %all-to-all-start.4 = ((f32[64,8,3]{1,2,0:T(4,128)}), f32[64,8,3]{1,2,0:T(4,128)S(1)}, u32[]{:S(2)}, u32[]{:S(2)}) async-start(f32[64,8,3]{1,2,0:T(4,128)} %copy.23), calls=%async_computation.4 | async-start | bytes 262144 | tf_op jit(solution)/shard_map/all_to_all | solution.py:139
  373.5 19.4 %all-to-all-start.8 = ((f32[64,1,4]{2,1,0:T(1,128)}), f32[64,1,4]{2,1,0:T(1,128)S(1)}, u32[]{:S(2)}, u32[]{:S(2)}) async-start(f32[64,1,4]{2,1,0:T(1,128)} %bitcast.3), calls=%async_computation.8 | async-start | bytes 65536 | tf_op jit(solution)/shard_map/all_to_all | solution.py:145
  392.9 14.2 %all-to-all-start.5 = ((f32[8,1,192]{2,1,0:T(1,128)}), f32[8,1,192]{2,1,0:T(1,128)S(1)}, u32[]{:S(2)}, u32[]{:S(2)}) async-start(f32[8,1,192]{2,1,0:T(1,128)} %reshape.195), calls=%async_computation.5 | async-start | bytes 16384 | tf_op jit(solution)/shard_map/all_to_all | solution.py:138
Sparse Core Ops, SparseCore 0:
  119.0 42.0 all-gather.2
where the time goes:
time: 424 us; the launch traced here: 422 us
  waiting for transfers between devices  184 us (43%)
  starting transfers between devices  77.6 us (18%)
  local copies, waits for them, and re-layouts  66.6 us (16%)
  blocking collectives  39.7 us (9%)
  other arithmetic  24.9 us (6%)
  between operations  13.7 us (3%)
  matrix products  13.3 us (3%)
    all_to_all x1, waiting for transfers between devices, local(): lax.all_to_all(small_send, 'dp', split_axis=0, concat_axis=0, tiled=True)  136 us
    all_gather x1, blocking collectives, local(): piece_ids = lax.all_gather(spread_ids, 'sub', axis=0, tiled=True)  39.7 us
    all_to_all x1, starting transfers between devices, local(): lax.all_to_all(large_tags, 'dp', split_axis=0, concat_axis=0, tiled=True)  19.3 us
    all_to_all x1, waiting for transfers between devices, local(): lax.all_to_all(planned_density, 'dp', split_axis=0, concat_axis=0, tiled=...  15 us
    reshape x2, local copies, waits for them, and re-layouts, local(): small_send.reshape(dp_count, sub_count, small_cap, feature_width)  14.7 us
    dot_general x4, matrix products, pair_terms(): lax.dot_general(left_rows, right_rows, (((1,), (1,)), ((), ())), preferre...  13.3 us
    all_to_all x1, waiting for transfers between devices, local(): lax.all_to_all(spread_density, 'dp', split_axis=0, concat_axis=0, tiled=T...  12.8 us
    all_to_all x1, starting transfers between devices, local(): lax.all_to_all(lax.all_to_all(small_tags, 'dp', split_axis=0, concat_axis...  12.1 us
  transfers between devices with their start and end apart: 10, of which 7 were waited for; matrix products, arithmetic and copies ran while one was open for 15% of the time, Pallas kernels for 0%

commit v1 on v0

--- a/solution.py
+++ b/solution.py
@@ -127,7 +127,12 @@
     places = jnp.arange(spread_total, dtype=jnp.int32)
     my_places = lax.axis_index("sub") * spread_total + places
     piece_rows = lax.all_gather(spread_flat, "sub", axis=0, tiled=True)
-    piece_ids = lax.all_gather(spread_ids, "sub", axis=0, tiled=True)
+    ring = [spread_ids]
+    for hop in range(7):
+        ring.append(lax.ppermute(ring[-1], "sub", [(dev, (dev + 1) % 8) for dev in range(8)]))
+    piece_ids = jnp.roll(
+        jnp.concatenate(ring[::-1], axis=0), (lax.axis_index("sub") + 1) * ring[0].shape[0], axis=0
+    )
     piece_places = jnp.arange(piece_rows.shape[0], dtype=jnp.int32)
     weights, same_cluster = pair_terms(
         spread_flat, spread_ids, my_places, piece_rows, piece_ids, piece_places

time: 424 us -> 416 us (0.981)
  blocking collectives: 39.7 us -> 0 us
  waiting for transfers between devices: 184 us -> 204 us
  starting transfers between devices: 77.6 us -> 90.2 us
    all_gather x1 -> x0, blocking collectives: 39.7 us -> none  [local(): piece_ids = lax.all_gather(spread_ids, 'sub', axis=0, tiled=True)]
    all_to_all x1, waiting for transfers between devices: 0.01 us -> 30.5 us  [local(): lax.all_to_all(lax.all_to_all(small_send, 'dp', split_axis=0, concat_axis...]
    all_to_all x1, waiting for transfers between devices: 136 us -> 119 us  [local(): lax.all_to_all(small_send, 'dp', split_axis=0, concat_axis=0, tiled=True)]
    ppermute x0 -> x7, starting transfers between devices: none -> 12.3 us  [local(): lax.ppermute(ring[-1], 'sub', [(dev, (dev + 1) % 8) for dev in range(8)])]
    ppermute x0 -> x7, waiting for transfers between devices: none -> 7.33 us  [local(): lax.ppermute(ring[-1], 'sub', [(dev, (dev + 1) % 8) for dev in range(8)])]
  transfers between devices with their start and end apart: 10 -> 17, of which waited for: 7 -> 12; matrix products, arithmetic and copies ran while one was open for 15% -> 15% of each run, Pallas kernels for 0% -> 0%
where the time goes in v1:
time: 416 us; the launch traced here: 415 us
  waiting for transfers between devices  204 us (49%)
  starting transfers between devices  90.2 us (22%)
  local copies, waits for them, and re-layouts  66.6 us (16%)
  other arithmetic  24.9 us (6%)
  between operations  13.8 us (3%)
  matrix products  13.3 us (3%)
    all_to_all x1, waiting for transfers between devices, local(): lax.all_to_all(small_send, 'dp', split_axis=0, concat_axis=0, tiled=True)  119 us
    all_to_all x1, waiting for transfers between devices, local(): lax.all_to_all(lax.all_to_all(small_send, 'dp', split_axis=0, concat_axis...  30.5 us
    all_to_all x1, starting transfers between devices, local(): lax.all_to_all(large_tags, 'dp', split_axis=0, concat_axis=0, tiled=True)  19.3 us
    reshape x2, local copies, waits for them, and re-layouts, local(): small_send.reshape(dp_count, sub_count, small_cap, feature_width)  14.7 us
    all_to_all x1, waiting for transfers between devices, local(): lax.all_to_all(planned_density, 'dp', split_axis=0, concat_axis=0, tiled=...  14.6 us
    dot_general x4, matrix products, pair_terms(): lax.dot_general(left_rows, right_rows, (((1,), (1,)), ((), ())), preferre...  13.3 us
    all_to_all x1, waiting for transfers between devices, local(): lax.all_to_all(spread_density, 'dp', split_axis=0, concat_axis=0, tiled=T...  12.8 us
    ppermute x7, starting transfers between devices, local(): lax.ppermute(ring[-1], 'sub', [(dev, (dev + 1) % 8) for dev in range(8)])  12.3 us
  transfers between devices with their start and end apart: 17, of which 12 were waited for; matrix products, arithmetic and copies ran while one was open for 15% of the time, Pallas kernels for 0%

profile of v1, /device:TPU:1, one launch (start us, length us, event | category | flops | bytes accessed | tf_op | source)
XLA Modules:
  0.0 415.2 jit_solution(3953129715769482599)
XLA Ops:
  13.8 19.3 %all-to-all-start.6 = ((s32[64,1,4]{2,1,0:T(1,128)}), s32[64,1,4]{2,1,0:T(1,128)S(1)}, u32[]{:S(2)}, u32[]{:S(2)}) async-start(s32[64,1,4]{2,1,0:T(1,128)} %bitcast), calls=%async_computation.6 | async-start | bytes 65536 | tf_op jit(solution)/shard_map/all_to_all | solution.py:104
  41.5 5.2 %all-to-all-done.6 = s32[64,1,4]{2,1,0:T(1,128)S(1)} async-done(((s32[64,1,4]{2,1,0:T(1,128)}), s32[64,1,4]{2,1,0:T(1,128)S(1)}, u32[]{:S(2)}, u32[]{:S(2)}) %all-to-all-start.6) | async-done | bytes 1056 | tf_op jit(solution)/shard_map/all_to_all | solution.py:104
  46.7 9.3 %all-to-all-start = ((s32[64,8,3]{1,2,0:T(4,128)}), s32[64,8,3]{1,2,0:T(4,128)S(1)}, u32[]{:S(2)}, u32[]{:S(2)}) async-start(s32[64,8,3]{1,2,0:T(4,128)} %copy.16), calls=%async_computation | async-start | bytes 262144 | tf_op jit(solution)/shard_map/all_to_all | solution.py:95
  56.0 5.7 %scatter_custom_fusion.3 = bf16[256,1024]{1,0:T(8,128)(2,1)S(1)} fusion(s32[1024]{0:T(1024)S(1)} %get-tuple-element.88, bf16[1024,1024]{1,0:T(8,128)(2,1)S(1)} %copy-done, f32[1024]{0:T(1024)S(1)} %add_rsqrt_fusion, bf16[]{:T(256)} %constant.108.clone.1), kind=kCustom, calls=%fused_computation.40 | custom fusion | flops 3145728 | bytes 2625538 | tf_op jit(solution)/shard_map/scatter | solution.py:79
  62.7 8.4 %all-to-all-done = s32[64,8,3]{1,2,0:T(4,128)S(1)} async-done(((s32[64,8,3]{1,2,0:T(4,128)}), s32[64,8,3]{1,2,0:T(4,128)S(1)}, u32[]{:S(2)}, u32[]{:S(2)}) %all-to-all-start) | async-done | bytes 6176 | tf_op jit(solution)/shard_map/all_to_all | solution.py:95
  71.1 6.4 %all-to-all-start.7 = ((bf16[64,4,1024]{2,1,0:T(4,128)(2,1)}), bf16[64,4,1024]{2,1,0:T(4,128)(2,1)S(1)}, u32[]{:S(2)}, u32[]{:S(2)}) async-start(bf16[64,4,1024]{2,1,0:T(4,128)(2,1)} %reshape.104), calls=%async_computation.7 | async-start | bytes 1048576 | tf_op jit(solution)/shard_map/all_to_all | solution.py:103
  77.5 7.8 %scatter_custom_fusion.1 = bf16[1536,1024]{1,0:T(8,128)(2,1)} fusion(s32[1024]{0:T(1024)S(1)} %get-tuple-element.90, bf16[]{:T(256)} %constant.108.clone.1, bf16[1024,1024]{1,0:T(8,128)(2,1)S(1)} %copy-done, f32[1024]{0:T(1024)S(1)} %add_rsqrt_fusion), kind=kCustom, calls=%fused_computation.37 | custom fusion | flops 3145728 | bytes 5246978 | tf_op jit(solution)/shard_map/scatter | solution.py:67
  85.3 9.1 %reshape.100 = bf16[64,8,3,1024]{3,2,1,0:T(4,128)(2,1)} reshape(bf16[1536,1024]{1,0:T(8,128)(2,1)} %scatter_custom_fusion.1) | data formatting | bytes 6291456 | tf_op jit(solution)/shard_map/reshape | solution.py:69
  94.4 5.6 %copy.19 = bf16[64,8,3,1024]{3,1,2,0:T(8,128)(2,1)} copy(bf16[64,8,3,1024]{3,2,1,0:T(4,128)(2,1)} %reshape.100) | data formatting | bytes 6291456 | tf_op jit(solution)/shard_map/reshape | solution.py:69
  100.0 6.3 %all-to-all-done.7 = bf16[64,4,1024]{2,1,0:T(4,128)(2,1)S(1)} async-done(((bf16[64,4,1024]{2,1,0:T(4,128)(2,1)}), bf16[64,4,1024]{2,1,0:T(4,128)(2,1)S(1)}, u32[]{:S(2)}, u32[]{:S(2)}) %all-to-all-start.7) | async-done | bytes 524320 | tf_op jit(solution)/shard_map/all_to_all | solution.py:103
  107.0 8.9 %all-to-all-start.2 = ((bf16[64,8,3,1024]{3,1,2,0:T(8,128)(2,1)}), bf16[64,8,3,1024]{3,1,2,0:T(8,128)(2,1)S(1)}, u32[]{:S(2)}, u32[]{:S(2)}) async-start(bf16[64,8,3,1024]{3,1,2,0:T(8,128)(2,1)} %copy.19), calls=%async_computation.2 | async-start | bytes 6291456 | tf_op jit(solution)/shard_map/all_to_all | solution.py:88
  135.2 119.1 %all-to-all-done.2 = bf16[64,8,3,1024]{3,1,2,0:T(8,128)(2,1)S(1)} async-done(((bf16[64,8,3,1024]{3,1,2,0:T(8,128)(2,1)}), bf16[64,8,3,1024]{3,1,2,0:T(8,128)(2,1)S(1)}, u32[]{:S(2)}, u32[]{:S(2)}) %all-to-all-start.2) | async-done | bytes 3145760 | tf_op jit(solution)/shard_map/all_to_all | solution.py:88
  254.3 12.1 %all-to-all-start.1 = ((s32[8,1,192]{2,1,0:T(1,128)}), s32[8,1,192]{2,1,0:T(1,128)S(1)}, u32[]{:S(2)}, u32[]{:S(2)}) async-start(s32[8,1,192]{2,1,0:T(1,128)} %reshape.187), calls=%async_computation.1 | async-start | bytes 16384 | tf_op jit(solution)/shard_map/all_to_all | solution.py:94
  285.6 30.5 %all-to-all-done.3 = bf16[64,8,3,1024]{3,0,2,1:T(8,128)(2,1)S(1)} async-done(((bf16[64,8,3,1024]{3,0,2,1:T(8,128)(2,1)}), bf16[64,8,3,1024]{3,0,2,1:T(8,128)(2,1)S(1)}, u32[]{:S(2)}, u32[]{:S(2)}) %all-to-all-start.3) | async-done | bytes 3145760 | tf_op jit(solution)/shard_map/all_to_all | solution.py:87
  316.1 4.6 %copy.21 = bf16[64,8,3,1024]{3,2,1,0:T(4,128)(2,1)} copy(bf16[64,8,3,1024]{3,0,2,1:T(8,128)(2,1)S(1)} %all-to-all-done.3) | data formatting | bytes 6291456 | tf_op jit(solution)/shard_map/all_to_all | solution.py:87
  320.7 7.5 %reshape.101 = bf16[1536,1024]{1,0:T(8,128)(2,1)S(1)} reshape(bf16[64,8,3,1024]{3,2,1,0:T(4,128)(2,1)} %copy.21) | data formatting | bytes 6291456 | tf_op jit(solution)/shard_map/reshape | solution.py:106
  328.3 15.6 %while.12 = (s32[]{:T(128)}, f32[3,512]{1,0:T(4,128)S(1)}, s32[3]{0:T(128)S(1)}, s32[1536]{0:T(1024)S(1)}, s32[64,8,3]{2,1,0:T(8,128)}, /*index=5*/bf16[1536,102...) while((s32[]{:T(128)}, f32[3,512]{1,0:T(4,128)S(1)}, ...), condition=%wide.wide.region_7.8_spmd.clone, body=%wide.wide.region_4.7_spmd.clone.sunk | while | flops 1619265024 | bytes 4237495 | solution.py:122
  345.2 5.6 %all-to-all-start.4 = ((f32[64,8,3]{1,2,0:T(4,128)}), f32[64,8,3]{1,2,0:T(4,128)S(1)}, u32[]{:S(2)}, u32[]{:S(2)}) async-start(f32[64,8,3]{1,2,0:T(4,128)} %copy.23), calls=%async_computation.4 | async-start | bytes 262144 | tf_op jit(solution)/shard_map/all_to_all | solution.py:144
  351.4 14.6 %all-to-all-done.4 = f32[64,8,3]{1,2,0:T(4,128)S(1)} async-done(((f32[64,8,3]{1,2,0:T(4,128)}), f32[64,8,3]{1,2,0:T(4,128)S(1)}, u32[]{:S(2)}, u32[]{:S(2)}) %all-to-all-start.4) | async-done | bytes 6176 | tf_op jit(solution)/shard_map/all_to_all | solution.py:144
  365.9 6.1 %all-to-all-start.8 = ((f32[64,1,4]{2,1,0:T(1,128)}), f32[64,1,4]{2,1,0:T(1,128)S(1)}, u32[]{:S(2)}, u32[]{:S(2)}) async-start(f32[64,1,4]{2,1,0:T(1,128)} %bitcast.2), calls=%async_computation.8 | async-start | bytes 65536 | tf_op jit(solution)/shard_map/all_to_all | solution.py:150
  372.9 12.8 %all-to-all-done.8 = f32[64,1,4]{2,1,0:T(1,128)S(1)} async-done(((f32[64,1,4]{2,1,0:T(1,128)}), f32[64,1,4]{2,1,0:T(1,128)S(1)}, u32[]{:S(2)}, u32[]{:S(2)}) %all-to-all-start.8) | async-done | bytes 1056 | tf_op jit(solution)/shard_map/all_to_all | solution.py:150
  385.7 6.0 %all-to-all-start.5 = ((f32[8,1,192]{2,1,0:T(1,128)}), f32[8,1,192]{2,1,0:T(1,128)S(1)}, u32[]{:S(2)}, u32[]{:S(2)}) async-start(f32[8,1,192]{2,1,0:T(1,128)} %reshape.189), calls=%async_computation.5 | async-start | bytes 16384 | tf_op jit(solution)/shard_map/all_to_all | solution.py:143
  393.1 6.8 %gather_fusion.1 = f32[1024]{0:T(1024)S(1)} fusion(f32[256]{0:T(256)S(1)} %reshape.106, s32[1024]{0:T(1024)S(1)} %get-tuple-element.87), kind=kCustom, calls=%fused_computation.1 | custom fusion | bytes 12288 | tf_op jit(solution)/shard_map/jit(_take)/gather | solution.py:152
  401.6 6.2 %gather_fusion = f32[1024]{0:T(1024)S(1)} fusion(f32[1536]{0:T(1024)S(1)} %reshape.103, s32[1024]{0:T(1024)S(1)} %get-tuple-element.89), kind=kCustom, calls=%fused_computation | custom fusion | bytes 12288 | tf_op jit(solution)/shard_map/jit(_take)/gather | solution.py:151
  (113 shorter events, 75.3 us)
Async XLA Ops:
  6.5 49.5 %copy-start = (bf16[1024,1024]{1,0:T(8,128)(2,1)S(1)}, bf16[1024,1024]{1,0:T(8,128)(2,1)}, u32[]{:S(2)}) copy-start(bf16[1024,1024]{1,0:T(8,128)(2,1)} %param.4) | copy-start | bytes 6291460
  13.8 32.9 %all-to-all-start.6 = ((s32[64,1,4]{2,1,0:T(1,128)}), s32[64,1,4]{2,1,0:T(1,128)S(1)}, u32[]{:S(2)}, u32[]{:S(2)}) async-start(s32[64,1,4]{2,1,0:T(1,128)} %bitcast), calls=%async_computation.6 | async-start | bytes 65536 | tf_op jit(solution)/shard_map/all_to_all | solution.py:104
  46.7 24.4 %all-to-all-start = ((s32[64,8,3]{1,2,0:T(4,128)}), s32[64,8,3]{1,2,0:T(4,128)S(1)}, u32[]{:S(2)}, u32[]{:S(2)}) async-start(s32[64,8,3]{1,2,0:T(4,128)} %copy.16), calls=%async_computation | async-start | bytes 262144 | tf_op jit(solution)/shard_map/all_to_all | solution.py:95
  71.1 35.1 %all-to-all-start.7 = ((bf16[64,4,1024]{2,1,0:T(4,128)(2,1)}), bf16[64,4,1024]{2,1,0:T(4,128)(2,1)S(1)}, u32[]{:S(2)}, u32[]{:S(2)}) async-start(bf16[64,4,1024]{2,1,0:T(4,128)(2,1)} %reshape.104), calls=%async_computation.7 | async-start | bytes 1048576 | tf_op jit(solution)/shard_map/all_to_all | solution.py:103
  106.2 0.8 copy-start.2
  107.0 147.2 %all-to-all-start.2 = ((bf16[64,8,3,1024]{3,1,2,0:T(8,128)(2,1)}), bf16[64,8,3,1024]{3,1,2,0:T(8,128)(2,1)S(1)}, u32[]{:S(2)}, u32[]{:S(2)}) async-start(bf16[64,8,3,1024]{3,1,2,0:T(8,128)(2,1)} %copy.19), calls=%async_computation.2 | async-start | bytes 6291456 | tf_op jit(solution)/shard_map/all_to_all | solution.py:88
  116.0 165.3 %all-gather.2.cloned.1.call-start = ((), (), s32[]{:S(2)}) async-start(), calls=%async_computation.9 | async-start | bytes 4718592 | tf_op jit(solution)/shard_map/all_gather | solution.py:129
  119.3 3.6 collective-permute-start
  122.9 3.0 collective-permute-start.1
  126.0 4.2 %collective-permute-start.2 = (s32[256]{0:T(256)S(1)}, s32[256]{0:T(256)S(1)}, u32[]{:S(2)}, u32[]{:S(2)}) collective-permute-start(s32[256]{0:T(256)S(1)} %collective-permute-done.1), channel_id=1, source_target_pairs={{0,1},{1,2},{2,3},{3,4},{4,5},{5,6},{6,7},{7,0},{8,9},{9,10},{10,1... | collective-permute-start | bytes 3080 | tf_op jit(solution)/shard_map/ppermute | solution.py:132
  130.2 4.2 %collective-permute-start.3 = (s32[256]{0:T(256)S(1)}, s32[256]{0:T(256)S(1)}, u32[]{:S(2)}, u32[]{:S(2)}) collective-permute-start(s32[256]{0:T(256)S(1)} %collective-permute-done.2), channel_id=1, source_target_pairs={{0,1},{1,2},{2,3},{3,4},{4,5},{5,6},{6,7},{7,0},{8,9},{9,10},{10,1... | collective-permute-start | bytes 3080 | tf_op jit(solution)/shard_map/ppermute | solution.py:132
  134.4 132.0 %collective-permute-start.4 = (s32[256]{0:T(256)S(1)}, s32[256]{0:T(256)S(1)}, u32[]{:S(2)}, u32[]{:S(2)}) collective-permute-start(s32[256]{0:T(256)S(1)} %collective-permute-done.3), channel_id=1, source_target_pairs={{0,1},{1,2},{2,3},{3,4},{4,5},{5,6},{6,7},{7,0},{8,9},{9,10},{10,1... | collective-permute-start | bytes 3080 | tf_op jit(solution)/shard_map/ppermute | solution.py:132
  254.3 20.2 %all-to-all-start.1 = ((s32[8,1,192]{2,1,0:T(1,128)}), s32[8,1,192]{2,1,0:T(1,128)S(1)}, u32[]{:S(2)}, u32[]{:S(2)}) async-start(s32[8,1,192]{2,1,0:T(1,128)} %reshape.187), calls=%async_computation.1 | async-start | bytes 16384 | tf_op jit(solution)/shard_map/all_to_all | solution.py:94
  266.4 2.4 collective-permute-start.5
  268.8 9.8 %collective-permute-start.6 = (s32[256]{0:T(256)S(1)}, s32[256]{0:T(256)S(1)}, u32[]{:S(2)}, u32[]{:S(2)}) collective-permute-start(s32[256]{0:T(256)S(1)} %collective-permute-done.5), channel_id=1, source_target_pairs={{0,1},{1,2},{2,3},{3,4},{4,5},{5,6},{6,7},{7,0},{8,9},{9,10},{10,1... | collective-permute-start | bytes 3080 | tf_op jit(solution)/shard_map/ppermute | solution.py:132
  274.4 41.7 %all-to-all-start.3 = ((bf16[64,8,3,1024]{3,0,2,1:T(8,128)(2,1)}), bf16[64,8,3,1024]{3,0,2,1:T(8,128)(2,1)S(1)}, u32[]{:S(2)}, u32[]{:S(2)}) async-start(bf16[64,8,3,1024]{3,0,2,1:T(8,128)(2,1)} %copy.20), calls=%async_computation.3 | async-start | bytes 6291456 | tf_op jit(solution)/shard_map/all_to_all | solution.py:87
  280.8 4.7 %copy-start.1 = (s32[64,8,3]{2,1,0:T(8,128)}, s32[64,8,3]{2,1,0:T(8,128)S(1)}, u32[]{:S(2)}) copy-start(s32[64,8,3]{2,1,0:T(8,128)S(1)} %copy.18) | copy-start | bytes 18436
  345.2 20.8 %all-to-all-start.4 = ((f32[64,8,3]{1,2,0:T(4,128)}), f32[64,8,3]{1,2,0:T(4,128)S(1)}, u32[]{:S(2)}, u32[]{:S(2)}) async-start(f32[64,8,3]{1,2,0:T(4,128)} %copy.23), calls=%async_computation.4 | async-start | bytes 262144 | tf_op jit(solution)/shard_map/all_to_all | solution.py:144
  365.9 19.8 %all-to-all-start.8 = ((f32[64,1,4]{2,1,0:T(1,128)}), f32[64,1,4]{2,1,0:T(1,128)S(1)}, u32[]{:S(2)}, u32[]{:S(2)}) async-start(f32[64,1,4]{2,1,0:T(1,128)} %bitcast.2), calls=%async_computation.8 | async-start | bytes 65536 | tf_op jit(solution)/shard_map/all_to_all | solution.py:150
  385.7 14.2 %all-to-all-start.5 = ((f32[8,1,192]{2,1,0:T(1,128)}), f32[8,1,192]{2,1,0:T(1,128)S(1)}, u32[]{:S(2)}, u32[]{:S(2)}) async-start(f32[8,1,192]{2,1,0:T(1,128)} %reshape.189), calls=%async_computation.5 | async-start | bytes 16384 | tf_op jit(solution)/shard_map/all_to_all | solution.py:143
Sparse Core Ops, SparseCore 0:
  119.0 42.0 all-gather.1
